TPU v7x, 32 devices: a whole 2x2x4 slice. The times are simulated.
32 devices in a mesh: fsdp: 16 (over z, x, core), seq: 2 (over y).
Axes of the slice: x: 2, y: 2, z: 4, core: 2. Of those that a mesh axis runs over, the one named last changes fastest.
Arguments:
- clips: bfloat16 [32, 1024, 1024], P('fsdp', 'seq'), may hold values from -6 to 6
- cotangent: bfloat16 [32, 1024, 1024], P('fsdp', 'seq'), may hold values from -6 to 6
- valid: int32 [32], P('fsdp'), may hold values 0 or 1
- norm1_gain: bfloat16 [1024], P('fsdp'), may hold values from 0.5 to 1.5
- norm1_bias: bfloat16 [1024], P('fsdp'), may hold values from -1.5 to 1.5
- query_weight: bfloat16 [1024, 1024], P('fsdp'), may hold values from -0.1875 to 0.1875
- key_weight: bfloat16 [1024, 1024], P('fsdp'), may hold values from -0.1875 to 0.1875
- value_weight: bfloat16 [1024, 1024], P('fsdp'), may hold values from -0.1875 to 0.1875
- query_bias: bfloat16 [1024], P('fsdp'), may hold values from -1.5 to 1.5
- value_bias: bfloat16 [1024], P('fsdp'), may hold values from -1.5 to 1.5
- proj_weight: bfloat16 [1024, 1024], P('fsdp'), may hold values from -2 to 2
- proj_bias: bfloat16 [1024], P('fsdp'), may hold values from -1.5 to 1.5
- norm2_gain: bfloat16 [1024], P('fsdp'), may hold values from 0.5 to 1.5
- norm2_bias: bfloat16 [1024], P('fsdp'), may hold values from -1.5 to 1.5
- fc1_weight: bfloat16 [1024, 4096], P('fsdp'), may hold values from -0.1875 to 0.1875
- fc1_bias: bfloat16 [4096], P('fsdp'), may hold values from -1.5 to 1.5
- fc2_weight: bfloat16 [4096, 1024], P('fsdp'), may hold values from -0.09375 to 0.09375
- fc2_bias: bfloat16 [1024], P('fsdp'), may hold values from -1.5 to 1.5
Outputs:
- layer_out: bfloat16 [32, 1024, 1024], P('fsdp', 'seq')
- grad_clips: float32 [32, 1024, 1024], P('fsdp', 'seq')
- grad_norm1_gain: float32 [1024], P('fsdp')
- grad_norm1_bias: float32 [1024], P('fsdp')
- grad_query_weight: float32 [1024, 1024], P('fsdp')
- grad_key_weight: float32 [1024, 1024], P('fsdp')
- grad_value_weight: float32 [1024, 1024], P('fsdp')
- grad_query_bias: float32 [1024], P('fsdp')
- grad_value_bias: float32 [1024], P('fsdp')
- grad_proj_weight: float32 [1024, 1024], P('fsdp')
- grad_proj_bias: float32 [1024], P('fsdp')
- grad_norm2_gain: float32 [1024], P('fsdp')
- grad_norm2_bias: float32 [1024], P('fsdp')
- grad_fc1_weight: float32 [1024, 4096], P('fsdp')
- grad_fc1_bias: float32 [4096], P('fsdp')
- grad_fc2_weight: float32 [4096, 1024], P('fsdp')
- grad_fc2_bias: float32 [1024], P('fsdp')
Inputs may be any that keep to these rules, and one draw needn't show every extreme that they name: Padding clips (valid 0) contribute nothing to any gradient.
All inputs are finite; a program needn't handle non-finite values. No bound on the sum of `valid` on one device may be relied on, other than what follows from the above.
Results may differ from a plain program's by a relative error of at most 0.023.
Values may be sent and summed in bfloat16 or wider, within the bound.
A program may use at most 256 MiB of HBM per device.

v0:
```python
import functools
import jax
import jax.numpy as jnp
from jax import lax
from jax.experimental import pallas as pl
from jax.experimental.pallas import tpu as pltpu
from jax.sharding import PartitionSpec as P

H = 16
QBLK = 512


norm_eps = 1e-06
root_half = 0.7071067811865476
inv_root_tau = 0.3989422804014327


def matmul(left, right):
    return jnp.dot(left, right, preferred_element_type=jnp.float32)


def matmul_nt(left, right):
    return lax.dot_general(
        left, right, (((1,), (1,)), ((), ())), preferred_element_type=jnp.float32
    )


def matmul_tn(left, right):
    return lax.dot_general(
        left, right, (((0,), (0,)), ((), ())), preferred_element_type=jnp.float32
    )


def layer_norm(values_in, gain, shift):
    row_mean = jnp.mean(values_in, axis=-1, keepdims=True)
    centred = values_in - row_mean
    inverse = lax.rsqrt(jnp.mean(centred * centred, axis=-1, keepdims=True) + norm_eps)
    scaled = centred * inverse
    return (scaled * gain + shift, scaled, inverse)


def layer_norm_back(upstream, scaled, inverse, gain):
    dscaled = upstream * gain
    inner = (
        dscaled
        - jnp.mean(dscaled, axis=-1, keepdims=True)
        - scaled * jnp.mean(dscaled * scaled, axis=-1, keepdims=True)
    )
    return (inverse * inner, jnp.sum(upstream * scaled, axis=0), jnp.sum(upstream, axis=0))


def gelu_value(pre_act):
    return 0.5 * pre_act * (1.0 + lax.erf(pre_act * root_half))


def gelu_slope(pre_act):
    return 0.5 * (1.0 + lax.erf(pre_act * root_half)) + pre_act * inv_root_tau * jnp.exp(
        -0.5 * pre_act * pre_act
    )


def attend(queries, keys_all, values_all, head_count):
    length = queries.shape[0]
    head_width = queries.shape[1] // head_count
    score_scale = head_width ** (-0.5)
    query_heads = queries.reshape(length // QBLK, QBLK, head_count, head_width)
    key_heads = keys_all.reshape(length, head_count, head_width)
    value_heads = values_all.reshape(length, head_count, head_width)

    def one_block(query_rows):
        scores = (
            jnp.einsum("qhd,khd->hqk", query_rows, key_heads, preferred_element_type=jnp.float32)
            * score_scale
        )
        peak = jnp.max(scores, axis=-1, keepdims=True)
        raised = jnp.exp(scores - peak)
        row_total = jnp.sum(raised, axis=-1, keepdims=True)
        weights = (raised / row_total).astype(jnp.bfloat16)
        mixed = jnp.einsum("hqk,khd->qhd", weights, value_heads, preferred_element_type=jnp.float32)
        return (mixed.astype(jnp.bfloat16), (peak + jnp.log(row_total))[:, :, 0])

    mixed, log_totals = lax.map(one_block, query_heads)
    return (mixed.reshape(length, head_count * head_width), log_totals)


def attend_back(queries, keys_all, values_all, log_totals, upstream, head_count):
    length = queries.shape[0]
    head_width = queries.shape[1] // head_count
    score_scale = head_width ** (-0.5)
    query_heads = queries.reshape(length // QBLK, QBLK, head_count, head_width)
    upstream_heads = upstream.reshape(length // QBLK, QBLK, head_count, head_width)
    key_heads = keys_all.reshape(length, head_count, head_width)
    value_heads = values_all.reshape(length, head_count, head_width)

    def one_block(running, block_item):
        key_grad, value_grad = running
        query_rows, log_rows, grad_rows = block_item
        scores = (
            jnp.einsum("qhd,khd->hqk", query_rows, key_heads, preferred_element_type=jnp.float32)
            * score_scale
        )
        weights = jnp.exp(scores - log_rows[:, :, None])
        weights_low = weights.astype(jnp.bfloat16)
        grad_weights = jnp.einsum(
            "qhd,khd->hqk", grad_rows, value_heads, preferred_element_type=jnp.float32
        )
        inner = jnp.sum(grad_weights * weights, axis=-1, keepdims=True)
        grad_scores = (weights * (grad_weights - inner)).astype(jnp.bfloat16)
        query_grad = (
            jnp.einsum("hqk,khd->qhd", grad_scores, key_heads, preferred_element_type=jnp.float32)
            * score_scale
        )
        key_grad = (
            key_grad
            + jnp.einsum(
                "hqk,qhd->khd", grad_scores, query_rows, preferred_element_type=jnp.float32
            )
            * score_scale
        )
        value_grad = value_grad + jnp.einsum(
            "hqk,qhd->khd", weights_low, grad_rows, preferred_element_type=jnp.float32
        )
        return ((key_grad, value_grad), query_grad.astype(jnp.bfloat16))

    zeros_heads = jnp.zeros((length, head_count, head_width), jnp.float32)
    (key_grad, value_grad), query_grad = lax.scan(
        one_block, (zeros_heads, zeros_heads), (query_heads, log_totals, upstream_heads)
    )
    width_all = head_count * head_width
    return (
        query_grad.reshape(length, width_all),
        key_grad.reshape(length, width_all).astype(jnp.bfloat16),
        value_grad.reshape(length, width_all).astype(jnp.bfloat16),
    )


def fetch(shards):
    return (
        lax.all_gather(shards[0], "fsdp", axis=0, tiled=True),
        lax.all_gather(shards[1], "fsdp", axis=0, tiled=True),
        lax.all_gather(shards[2], "fsdp", axis=0, tiled=True),
        lax.all_gather(shards[3], "fsdp", axis=0, tiled=True),
        lax.all_gather(shards[4], "fsdp", axis=0, tiled=True),
        lax.all_gather(shards[5], "fsdp", axis=0, tiled=True),
        lax.all_gather(shards[6], "fsdp", axis=0, tiled=True),
        lax.all_gather(shards[7], "fsdp", axis=0, tiled=True),
        lax.all_gather(shards[8], "fsdp", axis=0, tiled=True),
        lax.all_gather(shards[9], "fsdp", axis=0, tiled=True),
        lax.all_gather(shards[10], "fsdp", axis=0, tiled=True),
        lax.all_gather(shards[11], "fsdp", axis=0, tiled=True),
        lax.all_gather(shards[12], "fsdp", axis=0, tiled=True),
        lax.all_gather(shards[13], "fsdp", axis=0, tiled=True),
        lax.all_gather(shards[14], "fsdp", axis=0, tiled=True),
    )


def settle(grads):
    shares = (
        lax.psum_scatter(
            grads[0].astype(jnp.bfloat16), "fsdp", scatter_dimension=0, tiled=True
        ).astype(jnp.float32),
        lax.psum_scatter(
            grads[1].astype(jnp.bfloat16), "fsdp", scatter_dimension=0, tiled=True
        ).astype(jnp.float32),
        lax.psum_scatter(
            grads[2].astype(jnp.bfloat16), "fsdp", scatter_dimension=0, tiled=True
        ).astype(jnp.float32),
        lax.psum_scatter(
            grads[3].astype(jnp.bfloat16), "fsdp", scatter_dimension=0, tiled=True
        ).astype(jnp.float32),
        lax.psum_scatter(
            grads[4].astype(jnp.bfloat16), "fsdp", scatter_dimension=0, tiled=True
        ).astype(jnp.float32),
        lax.psum_scatter(
            grads[5].astype(jnp.bfloat16), "fsdp", scatter_dimension=0, tiled=True
        ).astype(jnp.float32),
        lax.psum_scatter(
            grads[6].astype(jnp.bfloat16), "fsdp", scatter_dimension=0, tiled=True
        ).astype(jnp.float32),
        lax.psum_scatter(
            grads[7].astype(jnp.bfloat16), "fsdp", scatter_dimension=0, tiled=True
        ).astype(jnp.float32),
        lax.psum_scatter(
            grads[8].astype(jnp.bfloat16), "fsdp", scatter_dimension=0, tiled=True
        ).astype(jnp.float32),
        lax.psum_scatter(
            grads[9].astype(jnp.bfloat16), "fsdp", scatter_dimension=0, tiled=True
        ).astype(jnp.float32),
        lax.psum_scatter(
            grads[10].astype(jnp.bfloat16), "fsdp", scatter_dimension=0, tiled=True
        ).astype(jnp.float32),
        lax.psum_scatter(
            grads[11].astype(jnp.bfloat16), "fsdp", scatter_dimension=0, tiled=True
        ).astype(jnp.float32),
        lax.psum_scatter(
            grads[12].astype(jnp.bfloat16), "fsdp", scatter_dimension=0, tiled=True
        ).astype(jnp.float32),
        lax.psum_scatter(
            grads[13].astype(jnp.bfloat16), "fsdp", scatter_dimension=0, tiled=True
        ).astype(jnp.float32),
        lax.psum_scatter(
            grads[14].astype(jnp.bfloat16), "fsdp", scatter_dimension=0, tiled=True
        ).astype(jnp.float32),
    )
    return (
        lax.psum(shares[0].astype(jnp.bfloat16), "seq").astype(jnp.float32),
        lax.psum(shares[1].astype(jnp.bfloat16), "seq").astype(jnp.float32),
        lax.psum(shares[2].astype(jnp.bfloat16), "seq").astype(jnp.float32),
        lax.psum(shares[3].astype(jnp.bfloat16), "seq").astype(jnp.float32),
        lax.psum(shares[4].astype(jnp.bfloat16), "seq").astype(jnp.float32),
        lax.psum(shares[5].astype(jnp.bfloat16), "seq").astype(jnp.float32),
        lax.psum(shares[6].astype(jnp.bfloat16), "seq").astype(jnp.float32),
        lax.psum(shares[7].astype(jnp.bfloat16), "seq").astype(jnp.float32),
        lax.psum(shares[8].astype(jnp.bfloat16), "seq").astype(jnp.float32),
        lax.psum(shares[9].astype(jnp.bfloat16), "seq").astype(jnp.float32),
        lax.psum(shares[10].astype(jnp.bfloat16), "seq").astype(jnp.float32),
        lax.psum(shares[11].astype(jnp.bfloat16), "seq").astype(jnp.float32),
        lax.psum(shares[12].astype(jnp.bfloat16), "seq").astype(jnp.float32),
        lax.psum(shares[13].astype(jnp.bfloat16), "seq").astype(jnp.float32),
        lax.psum(shares[14].astype(jnp.bfloat16), "seq").astype(jnp.float32),
    )


def one_clip(clip_in, clip_cot, clip_flag, gathered, head_count):
    (
        norm1_gain,
        norm1_bias,
        query_weight,
        key_weight,
        value_weight,
        query_bias,
        value_bias,
        proj_weight,
        proj_bias,
        norm2_gain,
        norm2_bias,
        fc1_weight,
        fc1_bias,
        fc2_weight,
        fc2_bias,
    ) = gathered
    gain_one = norm1_gain.astype(jnp.float32)
    gain_two = norm2_gain.astype(jnp.float32)
    tokens_in = clip_in.astype(jnp.float32)
    normed, scaled_one, inverse_one = layer_norm(
        tokens_in, gain_one, norm1_bias.astype(jnp.float32)
    )
    normed_low = normed.astype(jnp.bfloat16)
    queries = (matmul(normed_low, query_weight) + query_bias.astype(jnp.float32)).astype(
        jnp.bfloat16
    )
    keys_all = matmul(normed_low, key_weight).astype(jnp.bfloat16)
    values_all = (matmul(normed_low, value_weight) + value_bias.astype(jnp.float32)).astype(
        jnp.bfloat16
    )
    query_heads, key_heads, value_heads = (
        lax.all_to_all(queries, "seq", split_axis=1, concat_axis=0, tiled=True),
        lax.all_to_all(keys_all, "seq", split_axis=1, concat_axis=0, tiled=True),
        lax.all_to_all(values_all, "seq", split_axis=1, concat_axis=0, tiled=True),
    )
    mixed_heads, log_totals = attend(query_heads, key_heads, value_heads, head_count)
    attended = lax.all_to_all(mixed_heads, "seq", split_axis=0, concat_axis=1, tiled=True)
    middle = tokens_in + matmul(attended, proj_weight) + proj_bias.astype(jnp.float32)
    normed_two, scaled_two, inverse_two = layer_norm(
        middle, gain_two, norm2_bias.astype(jnp.float32)
    )
    normed_two_low = normed_two.astype(jnp.bfloat16)
    hidden_pre = matmul(normed_two_low, fc1_weight) + fc1_bias.astype(jnp.float32)
    hidden_low = gelu_value(hidden_pre).astype(jnp.bfloat16)
    output = middle + matmul(hidden_low, fc2_weight) + fc2_bias.astype(jnp.float32)
    grad_out = clip_cot.astype(jnp.float32) * clip_flag.astype(jnp.float32)
    grad_mlp = grad_out.astype(jnp.bfloat16)
    grad_fc2_weight = matmul_tn(hidden_low, grad_mlp)
    grad_fc2_bias = jnp.sum(grad_mlp.astype(jnp.float32), axis=0)
    grad_pre = (matmul_nt(grad_mlp, fc2_weight) * gelu_slope(hidden_pre)).astype(jnp.bfloat16)
    grad_fc1_weight = matmul_tn(normed_two_low, grad_pre)
    grad_fc1_bias = jnp.sum(grad_pre.astype(jnp.float32), axis=0)
    grad_norm_two = matmul_nt(grad_pre, fc1_weight)
    grad_ln_two, grad_norm2_gain, grad_norm2_bias = layer_norm_back(
        grad_norm_two, scaled_two, inverse_two, gain_two
    )
    grad_middle = grad_out + grad_ln_two
    grad_branch = grad_middle.astype(jnp.bfloat16)
    grad_proj_weight = matmul_tn(attended, grad_branch)
    grad_proj_bias = jnp.sum(grad_branch.astype(jnp.float32), axis=0)
    grad_att = matmul_nt(grad_branch, proj_weight).astype(jnp.bfloat16)
    grad_att_heads = lax.all_to_all(grad_att, "seq", split_axis=1, concat_axis=0, tiled=True)
    query_grad, key_grad, value_grad = attend_back(
        query_heads, key_heads, value_heads, log_totals, grad_att_heads, head_count
    )
    grad_queries, grad_keys, grad_values = (
        lax.all_to_all(query_grad, "seq", split_axis=0, concat_axis=1, tiled=True),
        lax.all_to_all(key_grad, "seq", split_axis=0, concat_axis=1, tiled=True),
        lax.all_to_all(value_grad, "seq", split_axis=0, concat_axis=1, tiled=True),
    )
    grad_query_weight = matmul_tn(normed_low, grad_queries)
    grad_key_weight = matmul_tn(normed_low, grad_keys)
    grad_value_weight = matmul_tn(normed_low, grad_values)
    grad_query_bias = jnp.sum(grad_queries.astype(jnp.float32), axis=0)
    grad_value_bias = jnp.sum(grad_values.astype(jnp.float32), axis=0)
    grad_norm_one = (
        matmul_nt(grad_queries, query_weight)
        + matmul_nt(grad_keys, key_weight)
        + matmul_nt(grad_values, value_weight)
    )
    grad_ln_one, grad_norm1_gain, grad_norm1_bias = layer_norm_back(
        grad_norm_one, scaled_one, inverse_one, gain_one
    )
    grad_in = grad_middle + grad_ln_one
    grads = (
        grad_norm1_gain,
        grad_norm1_bias,
        grad_query_weight,
        grad_key_weight,
        grad_value_weight,
        grad_query_bias,
        grad_value_bias,
        grad_proj_weight,
        grad_proj_bias,
        grad_norm2_gain,
        grad_norm2_bias,
        grad_fc1_weight,
        grad_fc1_bias,
        grad_fc2_weight,
        grad_fc2_bias,
    )
    return (output.astype(jnp.bfloat16), grad_in, grads)


def body(
    clips,
    cotangent,
    valid,
    norm1_gain,
    norm1_bias,
    query_weight,
    key_weight,
    value_weight,
    query_bias,
    value_bias,
    proj_weight,
    proj_bias,
    norm2_gain,
    norm2_bias,
    fc1_weight,
    fc1_bias,
    fc2_weight,
    fc2_bias,
):
    shards = (
        norm1_gain,
        norm1_bias,
        query_weight,
        key_weight,
        value_weight,
        query_bias,
        value_bias,
        proj_weight,
        proj_bias,
        norm2_gain,
        norm2_bias,
        fc1_weight,
        fc1_bias,
        fc2_weight,
        fc2_bias,
    )
    slot_count = clips.shape[0]
    head_count = H // lax.axis_size("seq")
    summed = None
    outputs = []
    grad_list = []
    for batch_slot in range(slot_count):
        gathered = fetch(shards)
        output, grad_in, grads = one_clip(
            clips[batch_slot], cotangent[batch_slot], valid[batch_slot], gathered, head_count
        )
        summed = (
            grads
            if summed is None
            else tuple((older + newer for older, newer in zip(summed, grads)))
        )
        outputs.append(output)
        grad_list.append(grad_in)
    summed = settle(summed)
    return (
        jnp.stack(outputs),
        jnp.stack(grad_list),
        summed[0],
        summed[1],
        summed[2],
        summed[3],
        summed[4],
        summed[5],
        summed[6],
        summed[7],
        summed[8],
        summed[9],
        summed[10],
        summed[11],
        summed[12],
        summed[13],
        summed[14],
    )


T, D, FF, NTILE = 1024, 1024, 4096, 8

log2_e = 1.4426950408889634
HD = 64
F32, BF16 = jnp.float32, jnp.bfloat16
ANY = pl.BlockSpec(memory_space=pl.ANY)


def dot(left, right, cl=1, cr=0):
    return lax.dot_general(left, right, (((cl,), (cr,)), ((), ())), preferred_element_type=F32)


def split3(v):
    hi = v.astype(BF16)
    r = v - hi.astype(F32)
    md = r.astype(BF16)
    lo = (r - md.astype(F32)).astype(BF16)
    return hi, md, lo


def aug_rows(v):
    hi, md, lo = split3(v)
    z = jnp.zeros((13, v.shape[1]), BF16)
    return jnp.concatenate([hi, md, lo, z], axis=0)


def ln_back(up, v, gain):
    m = jnp.mean(v, axis=-1, keepdims=True)
    d = v - m
    r = lax.rsqrt(jnp.mean(d * d, axis=-1, keepdims=True) + norm_eps)
    xh = d * r
    s = up * gain
    back = r * (s - jnp.mean(s, axis=-1, keepdims=True) - xh * jnp.mean(s * xh, axis=-1, keepdims=True))
    return back, jnp.sum(up * xh, axis=0, keepdims=True), jnp.sum(up, axis=0, keepdims=True)


def bwd_head(h, qkvt, ot, dot_v, lse_v):
    T = ot.shape[1]
    qb = T // 2
    scale = HD ** -0.5
    r = pl.multiple_of(h * HD, HD)
    rows = pl.ds(r, HD)
    ones = jnp.ones((16, T), BF16)
    kh = qkvt[1, rows, :]
    ka = jnp.concatenate([kh, ones], axis=0)
    va = jnp.concatenate([qkvt[2, rows, :], ones], axis=0)
    dk = dv = None
    for b in range(2):
        cols = slice(b * qb, (b + 1) * qb)
        qh = qkvt[0, rows, cols] * jnp.asarray(scale, BF16)
        do = dot_v[rows, cols]
        delta = jnp.sum(do.astype(F32) * ot[rows, cols].astype(F32), axis=0, keepdims=True)
        qa = jnp.concatenate([qh, aug_rows(-lse_v[pl.ds(h, 1), cols])], axis=0)
        da = jnp.concatenate([do, aug_rows(-delta)], axis=0)
        p = jnp.exp2(dot(qa, ka, 0, 0) * log2_e)
        ds = (p * dot(da, va, 0, 0)).astype(BF16)
        ndv = dot(do, p.astype(BF16))
        ndk = dot(qh, ds)
        dv = ndv if dv is None else dv + ndv
        dk = ndk if dk is None else dk + ndk
        qkvt[0, rows, cols] = (dot(kh, ds, 1, 1) * scale).astype(BF16)
    qkvt[1, rows, :] = dk.astype(BF16)
    qkvt[2, rows, :] = dv.astype(BF16)


MESH = pl.DeviceIdType.MESH


class Place:
    def __init__(self, size):
        f = lax.axis_index("fsdp")
        self.f, self.core, chip = f, f % 2, f // 2
        self.deep, self.count = size // 4, size // 2
        x, z = chip % 2, chip // 2
        self.pos = z + x * (2 * self.deep - 1 - 2 * z)
        self.mate = f + 1 - 2 * self.core
        self.y = lax.axis_index("seq")

    def chip(self, off):
        pos = (self.pos + self.count + off) % self.count
        hi = pos // self.deep
        return 2 * (pos + hi * (2 * self.deep - 1 - 2 * pos)) + hi

    def side(self, d):
        return {"fsdp": 2 * self.chip((1, -1)[d]) + self.core}

    def partner(self):
        return {"fsdp": self.mate}

    def across(self):
        return {"seq": 1 - self.y}

    def barrier(self):
        sem = pltpu.get_barrier_semaphore()
        for dev in (self.side(0), self.side(1), self.partner(), self.across()):
            pl.semaphore_signal(sem, inc=1, device_id=dev, device_id_type=MESH)
        pl.semaphore_wait(sem, 4)


def remote(src, dst, ss, rs, dev):
    return pltpu.make_async_remote_copy(src_ref=src, dst_ref=dst, send_sem=ss, recv_sem=rs, device_id=dev, device_id_type=MESH)


class Gather:
    def __init__(self, place, view, rsem, psem):
        self.pl, self.view, self.rsem, self.psem = place, view, rsem, psem
        self.last = place.count // 2 - 1

    def part(self, d, s):
        return d if s == self.last else 2

    def block(self, d, s, ahead):
        k = s + ahead
        return self.pl.chip(-k if d == 0 else k)

    def ring(self, d, s, ahead=0):
        v = self.view(2 * self.block(d, s, ahead) + self.pl.core, self.part(d, s))
        return remote(v, v, self.rsem.at[0, d, s], self.rsem.at[1, d, s], self.pl.side(d))

    def mate(self, slot, chip, part, core):
        v = self.view(2 * chip + core, part)
        return remote(v, v, self.psem.at[0, slot], self.psem.at[1, slot], self.pl.partner())

    def slots(self, s):
        return [(1 + 2 * s + d, self.block(d, s, 1), self.part(d, s)) for d in range(2)]

    def start(self):
        for d in range(2):
            self.ring(d, 0).start()
        self.mate(0, self.pl.chip(0), 2, self.pl.core).start()

    def step(self, s):
        for d in range(2):
            self.ring(d, s, 1).wait_recv()
            if s < self.last:
                self.ring(d, s + 1).start()
        for slot, chip, part in self.slots(s):
            self.mate(slot, chip, part, self.pl.core).start()

    def own_mate(self):
        self.mate(0, self.pl.chip(0), 2, 1 - self.pl.core).wait_recv()

    def step_mate(self, s):
        for slot, chip, part in self.slots(s):
            self.mate(slot, chip, part, 1 - self.pl.core).wait_recv()

    def all_mates(self):
        self.own_mate()
        for s in range(self.last + 1):
            self.step_mate(s)

    def drain(self):
        for s in range(self.last + 1):
            for d in range(2):
                self.ring(d, s).wait_send()
            for slot, chip, part in self.slots(s):
                self.mate(slot, chip, part, self.pl.core).wait_send()
        self.mate(0, self.pl.chip(0), 2, self.pl.core).wait_send()


class GatherY(Gather):
    def __init__(self, place, half, whole, rsem, psem, qsem, asem):
        super().__init__(place, lambda f, part: half(f, part, place.y), rsem, psem)
        self.half, self.whole, self.qsem, self.asem = half, whole, qsem, asem

    def mate(self, slot, chip, part, core):
        if slot:
            return super().mate(slot, chip, part, core)
        v = self.whole(2 * chip + core)
        return remote(v, v, self.psem.at[0, 0], self.psem.at[1, 0], self.pl.partner())

    def over(self, slot, chip, part, y):
        v = self.half(2 * chip + self.pl.core, part, y)
        return remote(v, v, self.asem.at[0, slot], self.asem.at[1, slot], self.pl.across())

    def relay(self, slot, chip, part, core):
        v = self.half(2 * chip + core, part, 1 - self.pl.y)
        return remote(v, v, self.qsem.at[0, slot], self.qsem.at[1, slot], self.pl.partner())

    def step(self, s):
        for d in range(2):
            self.ring(d, s, 1).wait_recv()
            if s < self.last:
                self.ring(d, s + 1).start()
        for slot, chip, part in self.slots(s):
            self.over(slot, chip, part, self.pl.y).start()
            self.mate(slot, chip, part, self.pl.core).start()

    def step_over(self, s):
        for slot, chip, part in self.slots(s):
            self.over(slot, chip, part, 1 - self.pl.y).wait_recv()
            self.relay(slot, chip, part, self.pl.core).start()

    def step_mate(self, s):
        super().step_mate(s)
        for slot, chip, part in self.slots(s):
            self.relay(slot, chip, part, 1 - self.pl.core).wait_recv()

    def drain(self):
        super().drain()
        for s in range(self.last + 1):
            for slot, chip, part in self.slots(s):
                self.over(slot, chip, part, self.pl.y).wait_send()
                self.relay(slot, chip, part, self.pl.core).wait_send()


def fwd_body(size, clips, cot, sml, wq, wk, wv, wp, w1, w2,
             out_o, cot_o, x_o, sm_o, wqkv_o, wp_o, w1_o, w2_o, n1t_o, qkvt_o, ot_o, lse_o, mid_o, n2_o, h_o, g_o,
             x_v, smb, sm_v, wqkv_v, wp_v, w1_v, w2_v, n1t, qkvt, ot, lse_v, mid, n2, acc, hst, gst, b1_v, smt,
             rsem, psem, qsem, asem, xsem, lsem, osem, tsem):
    here = Place(size)
    T, D = x_v.shape
    FF = w1_v.shape[1]
    tile = hst.shape[2]
    heads = D // HD
    half = T // 2
    nd, nf = D // size, FF // size
    y = here.y
    ymine = pl.ds(pl.multiple_of(y * half, half), half)
    yother = pl.ds(pl.multiple_of((1 - y) * half, half), half)

    def local(a, b, i):
        return pltpu.make_async_copy(a, b, lsem.at[i])

    def rows(ref, n, lead):
        def view(f, part):
            k = n if part == 2 else n // 2
            at = pl.ds(pl.multiple_of(f * n + (n // 2 if part == 1 else 0), k), k)
            return ref.at[:, at, :] if lead else ref.at[at, :]
        return view

    def smview(f, part):
        if part == 2:
            return smb.at[f]
        return smb.at[f, :, part * (D // 2):(part + 1) * (D // 2)]

    def part_rows(ref, n, c0, w):
        def half_view(f, part, yy):
            k = n if part == 2 else n // 2
            at = pl.ds(pl.multiple_of(f * n + (n // 2 if part == 1 else 0), k), k)
            return ref.at[at, pl.ds(pl.multiple_of(c0 + yy * (w // 2), w // 2), w // 2)]

        def whole_view(f):
            return ref.at[pl.ds(pl.multiple_of(f * n, n), n), c0:c0 + w]

        return half_view, whole_view

    def first_rows(f, part):
        return rows(w1_v, nd, False)(f, part).at[:, 0:FF // 2]

    views = [smview, rows(wqkv_v, nd, True), rows(wp_v, nd, False), first_rows]
    ga, gq, gp, g1 = [Gather(here, v, rsem.at[i], psem.at[i]) for i, v in enumerate(views)]
    g3 = GatherY(here, *part_rows(w1_v, nd, FF // 2, FF // 2), rsem.at[4], psem.at[4], qsem.at[0], asem.at[0])
    g2 = GatherY(here, *part_rows(w2_v, nf, 0, D), rsem.at[5], psem.at[5], qsem.at[1], asem.at[1])
    own = pl.ds(pl.multiple_of(here.f * nd, nd), nd)
    ownf = pl.ds(pl.multiple_of(here.f * nf, nf), nf)
    loc = [local(sml, smb.at[here.f], 0)]
    loc += [local(w, wqkv_v.at[j, own, :], 1 + j) for j, w in enumerate((wq, wk, wv))]
    loc += [local(wp, wp_v.at[own, :], 4), local(w1, w1_v.at[own, :], 5), local(w2, w2_v.at[ownf, :], 6), local(clips.at[y], x_v.at[ymine, :], 7)]
    for c in loc:
        c.start()
    here.barrier()
    xsend = remote(clips.at[1 - y], x_v.at[ymine, :], xsem.at[0, 0], xsem.at[0, 1], here.across())
    xrecv = remote(clips.at[1 - y], x_v.at[yother, :], xsem.at[0, 0], xsem.at[0, 1], here.across())
    csend = remote(cot.at[1 - y], cot_o, xsem.at[1, 0], xsem.at[1, 1], here.across())
    xsend.start()
    csend.start()
    for c in loc[:4]:
        c.wait()
    ga.start()
    gq.start()
    for c in loc[4:]:
        c.wait()

    def ln1(i, c):
        r = pl.multiple_of(i * 256, 256)
        v = x_v[pl.ds(r, 256), :].astype(F32)
        m = jnp.mean(v, axis=-1, keepdims=True)
        d = v - m
        mid[pl.ds(r, 256), :] = d * lax.rsqrt(jnp.mean(d * d, axis=-1, keepdims=True) + norm_eps)
        return c

    per = half // 256
    lax.fori_loop(y * per, y * per + per, ln1, 0)
    for s in range(ga.last + 1):
        ga.step(s)
        gq.step(s)
        if s == ga.last - 1:
            gp.start()
            g1.start()
            g3.start()
    xrecv.wait_recv()
    lax.fori_loop((1 - y) * per, (1 - y) * per + per, ln1, 0)
    ga.all_mates()
    sm_v[...] = jnp.sum(smb[...].astype(F32), axis=0)
    smt[...] = jnp.transpose(sm_v[...])

    def ln1b(i, c):
        r = pl.multiple_of(i * 256, 256)
        n1t[:, pl.ds(r, 256)] = jnp.transpose((mid[pl.ds(r, 256), :] * sm_v[0:1, :] + sm_v[1:2, :]).astype(BF16))
        return c

    lax.fori_loop(0, T // 256, ln1b, 0)
    gq.all_mates()
    outs = []

    def save(a, b):
        c = pltpu.make_async_copy(a, b, osem.at[len(outs)])
        outs.append(c)
        c.start()

    save(wqkv_v, wqkv_o)
    save(x_v, x_o)
    save(sm_v, sm_o)
    save(n1t, n1t_o)
    hd = D // 2
    for j in range(3):
        for o in range(2):
            v = dot(wqkv_v[j, :, o * hd:(o + 1) * hd], n1t[...], 0, 0)
            if j != 1:
                v = v + smt[o * hd:(o + 1) * hd, (2 if j == 0 else 3):(3 if j == 0 else 4)]
            qkvt[j, o * hd:(o + 1) * hd, :] = v.astype(BF16)
    save(qkvt, qkvt_o)
    qb = T // 2
    ones = jnp.ones((16, T), BF16)

    def head(h, c):
        r = pl.multiple_of(h * HD, HD)
        kh = qkvt[1, pl.ds(r, HD), :]
        vh = jnp.concatenate([qkvt[2, pl.ds(r, HD), :], ones], axis=0)
        for b in range(2):
            qh = qkvt[0, pl.ds(r, HD), b * qb:(b + 1) * qb]
            s = dot(kh, qh, 0, 0)
            m = jnp.max(s, axis=0, keepdims=True)
            p = jnp.exp2((s - m) * (log2_e * HD ** -0.5)).astype(BF16)
            o = dot(vh, p)
            total = o[HD:HD + 1, :]
            ot[pl.ds(r, HD), b * qb:(b + 1) * qb] = (o[:HD, :] / total).astype(BF16)
            lse_v[pl.ds(h, 1), b * qb:(b + 1) * qb] = m * HD ** -0.5 + jnp.log(total)
        for s, n in enumerate((2, 8, 14)):
            @pl.when(h == n)
            def _(s=s):
                gp.step(s)
                g1.step(s)
                g3.step(s)
                if s:
                    g3.step_over(s - 1)
                if s == 2:
                    g2.start()
        return c

    lax.fori_loop(0, heads, head, 0)
    save(ot, ot_o)
    save(lse_v, lse_o)
    for s in range(3, gp.last + 1):
        gp.step(s)
    gp.all_mates()
    save(wp_v, wp_o)

    def proj(i, c):
        r = pl.multiple_of(i * 512, 512)
        v = dot(ot[:, pl.ds(r, 512)], wp_v[...], 0, 0) + x_v[pl.ds(r, 512), :].astype(F32) + sm_v[4:5, :]
        mid[pl.ds(r, 512), :] = v
        m = jnp.mean(v, axis=-1, keepdims=True)
        d = v - m
        s = d * lax.rsqrt(jnp.mean(d * d, axis=-1, keepdims=True) + norm_eps)
        n2[pl.ds(r, 512), :] = (s * sm_v[5:6, :] + sm_v[6:7, :]).astype(BF16)
        acc[pl.ds(r, 512), :] = v + sm_v[7:8, :]
        return c

    lax.fori_loop(0, T // 512, proj, 0)
    save(mid, mid_o)
    save(n2, n2_o)
    for k in range(FF // tile):
        kk = k * tile
        b1_v[k:k + 1, :] = sm_v[8 + kk // D:9 + kk // D, kk % D:kk % D + tile]
    for s in range(3, g1.last + 1):
        g1.step(s)
        g3.step(s)
        g3.step_over(s - 1)
    g3.step_over(g3.last)
    g2.step(0)
    g1.all_mates()
    g3.all_mates()
    g2.own_mate()
    save(w1_v, w1_o)
    saves = {}
    order = [0]
    for k in range(1, here.count // 2):
        order += [-k, k]
    order.append(here.count // 2)

    def tcp(k, slot, t):
        return pltpu.make_async_copy((hst, gst)[k].at[slot], (h_o, g_o)[k].at[t], tsem.at[k, slot])

    def wcp(j, t):
        at = pl.ds(pl.multiple_of(t * tile, tile), tile)
        return pltpu.make_async_copy(w2_v.at[at, :], w2_o.at[at, :], tsem.at[2, j])

    for j, off in enumerate(order):
        t = here.chip(off)
        slot = j % 2
        if j % 2 == 1:
            g2.step_over(j // 2)
            if j // 2 < g2.last:
                g2.step(j // 2 + 1)
            g2.step_mate(j // 2)
        wcp(j, t).start()
        if j >= 2:
            for k in range(2):
                tcp(k, slot, here.chip(order[j - 2])).wait()
        col = pl.multiple_of(t * tile, tile)

        def mlp(i, c, t=t, slot=slot, col=col):
            r = pl.multiple_of(i * 512, 512)
            u = dot(n2[pl.ds(r, 512), :], w1_v[:, pl.ds(col, tile)]) + b1_v[pl.ds(t, 1), :]
            cdf = 0.5 + 0.5 * lax.erf(u * root_half)
            hb = (u * cdf).astype(BF16)
            hst[slot, pl.ds(r, 512), :] = hb
            gst[slot, pl.ds(r, 512), :] = (cdf + (u * inv_root_tau) * jnp.exp2(u * u * (-0.5 * log2_e))).astype(BF16)
            acc[pl.ds(r, 512), :] += dot(hb, w2_v[pl.ds(col, tile), :])
            return c

        lax.fori_loop(0, T // 512, mlp, 0)
        for k in range(2):
            tcp(k, slot, t).start()
    for j in range(len(order) - 2, len(order)):
        for k in range(2):
            tcp(k, j % 2, here.chip(order[j])).wait()
    outs[3].wait()
    n1t[...] = acc[...].astype(BF16)
    save(n1t, out_o)
    for j, off in enumerate(order):
        wcp(j, here.chip(off)).wait()
    for i, c in enumerate(outs):
        if i != 3:
            c.wait()
    for g in (ga, gq, gp, g1, g3, g2):
        g.drain()
    xsend.wait_send()
    csend.wait_send()
    remote(cot.at[1 - y], cot_o, xsem.at[1, 0], xsem.at[1, 1], here.across()).wait_recv()


S = jax.ShapeDtypeStruct
V = pltpu.VMEM


def fwd_call(size, T, D, FF):
    tile = 2 * FF // size
    heads = D // HD
    small = (16, D)
    dma = pltpu.SemaphoreType.DMA
    steps = size // 4
    return pl.pallas_call(
        functools.partial(fwd_body, size),
        name="forward",
        in_specs=[ANY] * 9,
        out_specs=[ANY] * 16,
        out_shape=[S((T, D), BF16), S((T // 2, D), BF16), S((T, D), BF16), S(small, F32), S((3, D, D), BF16), S((D, D), BF16), S((D, FF), BF16), S((FF, D), BF16),
                   S((D, T), BF16), S((3, D, T), BF16), S((D, T), BF16), S((heads, T), F32), S((T, D), F32), S((T, D), BF16), S((FF // tile, T, tile), BF16), S((FF // tile, T, tile), BF16)],
        scratch_shapes=[V((T, D), BF16), V((size,) + small, BF16), V(small, F32), V((3, D, D), BF16), V((D, D), BF16), V((D, FF), BF16), V((FF, D), BF16),
                        V((D, T), BF16), V((3, D, T), BF16), V((D, T), BF16), V((heads, T), F32), V((T, D), F32), V((T, D), BF16), V((T, D), F32),
                        V((2, T, tile), BF16), V((2, T, tile), BF16), V((FF // tile, tile), F32), V((D, 16), F32),
                        dma((6, 2, 2, steps)), dma((6, 2, 2 * steps + 1)), dma((2, 2, 2 * steps + 1)), dma((2, 2, 2 * steps + 1)), dma((2, 2)), dma((8,)), dma((12,)), dma((3, max(2, FF // tile)))],
        compiler_params=pltpu.CompilerParams(vmem_limit_bytes=63 << 20, collective_id=0, has_side_effects=True),
    )


def fold(dst, *srcs):
    def one(q, c):
        if len(srcs) == 1:
            dst[q] = dst[q] + srcs[0][q]
            return c
        v = dst[q].astype(F32)
        for s in srcs:
            v = v + s[q].astype(F32)
        dst[q] = v.astype(dst.dtype)
        return c

    lax.fori_loop(0, dst.shape[0], one, 0)


def offset(j):
    odd = j % 2
    return odd * ((7 - j) // 2) - (1 - odd) * ((8 - j) // 2)


class Scatter:
    def __init__(self, here, land, rb, n, cols, msem, rsem, ysem, fin_o=None, y_o=None):
        self.pl, self.land, self.rb, self.n, self.cols = here, land, rb, n, cols
        self.msem, self.rsem, self.ysem, self.fin_o, self.y_o = msem, rsem, ysem, fin_o, y_o

    def cut(self, part):
        c0, w = self.cols
        return slice(c0, c0 + w) if part == 2 else slice(c0 + part * (w // 2), c0 + (part + 1) * (w // 2))

    def block(self, j, part=2):
        return self.land.at[j, 0:self.n, :, self.cut(part)]

    def came(self, d, s):
        return self.rb.at[d, s, 0:self.n, :, self.cut(d if s == 0 else 2)]

    def mate(self, j, src=None):
        dst = self.block(j)
        return remote(dst if src is None else src.at[:, :, self.cut(2)], dst, self.msem.at[0, j], self.msem.at[1, j], self.pl.partner())

    def settle(self, j, own):
        self.mate(j).wait_recv()
        fold(self.block(j), own.at[:, :, self.cut(2)])
        self.mate(j).wait_send()

    def ring(self, d, s):
        src = self.block(0, d) if s == 0 else self.block(2 * s - 1 + d)
        return remote(src, self.came(d, s), self.rsem.at[0, d, s], self.rsem.at[1, d, s], self.pl.side(d))

    def step(self, s):
        for d in range(2):
            if s:
                self.ring(d, s - 1).wait_recv()
                fold(self.block(2 * s - 1 + d, d if s == 1 else 2), self.came(d, s - 1))
            self.ring(d, s).start()

    def close(self):
        for d in range(2):
            self.ring(d, 3).wait_recv()
        fold(self.block(7), self.came(0, 3), self.came(1, 3))

    def view(self, ref):
        return ref.at[0:self.n, :, self.cut(2)]

    def over(self):
        return remote(self.block(7), self.view(self.y_o), self.ysem.at[0], self.ysem.at[1], self.pl.across())

    def keep(self):
        return pltpu.make_async_copy(self.block(7), self.view(self.fin_o), self.ysem.at[2])

    def finish(self):
        self.close()
        self.over().start()
        self.keep().start()

    def drain_ring(self):
        for s in range(4):
            for d in range(2):
                self.ring(d, s).wait_send()

    def drain(self):
        self.drain_ring()
        self.over().wait_send()
        self.keep().wait()


class Group:
    def __init__(self, *parts):
        self.parts = parts

    def send(self, j, src):
        for p in self.parts:
            p.mate(j, src).start()

    def settle(self, j, own):
        for p in self.parts:
            p.settle(j, own)

    def step(self, s):
        for p in self.parts:
            p.step(s)

    def finish(self):
        for p in self.parts:
            p.finish()

    def drain(self):
        for p in self.parts:
            p.drain()

    def arrive(self):
        for p in self.parts:
            p.over().wait_recv()


def bwd_body(size, valid, cotangent, cot_in, out, x, sm, wqkv, wp, w1, w2, n1t, qkvt, ot, lse, mid, n2, hs, gs,
             out_o, gx_o, gxr_o, dw2_o, dw2_y, dw1_o, dw1_y, dwp_o, dwp_y, dq_o, dq_y, sg_o,
             g_v, n2_v, gacc, h_v, pre_v, w1_v, w2_v, b1g, mid_v, qkvt_v, ot_v, lse_v, sm_v, sg_v, sgm_v, sgy_v,
             st_v, land_a, land_b, land_p, land_s, rb_a, rb_b, rb_p, rb_s,
             sem, tsem, wsem, mlsem, xsem, msem, rsem, ysem, ssem, gsem, free):
    here = Place(size)
    y, core = here.y, here.core
    half = T // 2
    ymine = pl.multiple_of(y * half, half)
    yother = pl.multiple_of((1 - y) * half, half)

    def cp(a, b, i):
        return pltpu.make_async_copy(a, b, sem.at[i])

    first = [cp(cotangent.at[y], g_v.at[pl.ds(ymine, half), :], 0), cp(cot_in, g_v.at[pl.ds(yother, half), :], 1), cp(n2, n2_v, 2), cp(sm, sm_v, 3)]
    later = [cp(qkvt, qkvt_v, 4), cp(ot, ot_v, 5), cp(lse, lse_v, 6)]
    last = [cp(x, h_v, 7), cp(n1t, w1_v, 8)]

    def chip(j):
        return here.chip(offset(j))

    def tl(t, s):
        c = pl.multiple_of(t * 512, 512)
        d = pl.multiple_of(s * 512, 512)
        return [
            pltpu.make_async_copy(hs.at[t], h_v.at[:, pl.ds(d, 512)], tsem.at[s, 0]),
            pltpu.make_async_copy(gs.at[t], pre_v.at[t], tsem.at[s, 1]),
            pltpu.make_async_copy(w1.at[:, pl.ds(c, 512)], w1_v.at[:, pl.ds(d, 512)], tsem.at[s, 2]),
            pltpu.make_async_copy(w2.at[pl.ds(c, 512), :], w2_v.at[pl.ds(d, 512), :], tsem.at[s, 3]),
        ]

    for c in first:
        c.start()
    for c in tl(chip(0), 0):
        c.start()
    for c in later:
        c.start()
    here.barrier()
    osend = remote(out.at[pl.ds(yother, half), :], out_o, gsem.at[0, 0], gsem.at[0, 1], here.across())
    osend.start()
    def scatter(i, land, rb, n, c0, w, fin_o, y_o):
        return Scatter(here, land, rb, n, (c0, w), msem.at[i], rsem.at[i], ysem.at[i], fin_o, y_o)

    s2 = Group(*[scatter(i, land_a, rb_a, 4, i * 512, 512, dw2_o, dw2_y) for i in range(2)])
    s1 = Group(*[scatter(2 + i, land_b, rb_b, 4, i * 512, 512, dw1_o, dw1_y) for i in range(2)])
    sp = Group(scatter(4, land_p, rb_p, 1, 0, D, dwp_o, dwp_y))
    qcols = ((0, 512), (512, 256), (768, 256))
    sq = [Group(scatter(5 + g, land_a, rb_a, 3, c0, w, dq_o, dq_y)) for g, (c0, w) in enumerate(qcols)]
    ss = Scatter(here, land_s, rb_s, 2, (0, 128), None, rsem.at[8], None)
    for c in first:
        c.wait()
    flag = valid[y].astype(F32)
    sg_v[...] = jnp.zeros_like(sg_v)

    def mask(i, c):
        r = pl.multiple_of(i * 256, 256)
        v = g_v[pl.ds(r, 256), :].astype(F32) * flag
        g_v[pl.ds(r, 256), :] = v.astype(BF16)
        sg_v[7:8, :] += jnp.sum(v, axis=0, keepdims=True)
        return c

    lax.fori_loop(0, T // 256, mask, 0)

    def st2(j, k):
        return st_v.at[0, pl.ds((j % 2) * 8 + k * 4, 4)]

    def tile(j, c):
        s = j % 2
        t = chip(j)

        @pl.when(j + 1 < NTILE)
        def _():
            for k in tl(chip(j + 1), 1 - s):
                k.start()

        for k in tl(t, s):
            k.wait()
        col = pl.ds(pl.multiple_of(s * 512, 512), 512)
        gb = g_v[...]
        st_v[0, pl.ds(s * 8, 8)] = dot(h_v[:, col], gb, 0, 0).astype(BF16).reshape(8, 64, D)
        s2.send(j, st2(j, 1 - core))
        pre = (dot(gb, w2_v[col, :], 1, 1) * pre_v[t].astype(F32)).astype(BF16)
        pre_v[t] = pre
        b1g[pl.ds(t, 1), :] = jnp.sum(pre.astype(F32), axis=0, keepdims=True)
        v = dot(pre, w1_v[:, col], 1, 1)

        @pl.when(j == 0)
        def _():
            gacc[...] = v

        @pl.when(j > 0)
        def _():
            gacc[...] += v

        s2.settle(j, st2(j, core))
        for k, n in enumerate((0, 2, 4)):
            @pl.when(j == n)
            def _(k=k):
                s2.step(k)

        return c

    lax.fori_loop(0, NTILE, tile, 0)
    for c in last:
        c.start()
    sg_v[8:16, 0:512] = b1g[...]

    def slots(q):
        return (2 * q + 7) % 8, 2 * q

    def st1(q, i, k):
        return st_v.at[1 + q % 2, pl.ds(i * 8 + k * 4, 4)]

    def settle1(q):
        for i, j in enumerate(slots(q)):
            s1.settle(j, st1(q, i, core))

    def pair1(q, c):
        at = [pl.ds(pl.multiple_of(chip(j) * 128, 128), 128) for j in slots(q)]
        left = jnp.concatenate([n2_v[:, a] for a in at], axis=1)
        for cb in range(4):
            for k in range(2):
                v = dot(left, pre_v[2 * cb + k], 0, 0).astype(BF16)
                for i in range(2):
                    for e in range(2):
                        st_v[1 + q % 2, i * 8 + e * 4 + cb, :, k * 512:(k + 1) * 512] = v[i * 128 + e * 64:i * 128 + e * 64 + 64]
        for i, j in enumerate(slots(q)):
            s1.send(j, st1(q, i, 1 - core))

        @pl.when(q > 0)
        def _():
            settle1(q - 1)

        @pl.when(q == 1)
        def _():
            s2.step(3)
            s1.step(0)

        return c

    lax.fori_loop(0, 4, pair1, 0)
    wpl = [pltpu.make_async_copy(wp.at[:, i * 512:(i + 1) * 512], pre_v.at[6 + i], wsem.at[6 + i]) for i in range(2)]
    wl = [pltpu.make_async_copy(wqkv.at[j, :, i * 512:(i + 1) * 512], pre_v.at[2 * j + i], wsem.at[2 * j + i]) for j in range(3) for i in range(2)]
    for c in wpl + wl:
        c.start()
    settle1(3)

    def ml(i, s):
        return pltpu.make_async_copy(mid.at[pl.ds(pl.multiple_of(i * 256, 256), 256), :], mid_v.at[s], mlsem.at[s])

    ml(0, 0).start()

    def ln2(i, c):
        r = pl.multiple_of(i * 256, 256)
        s = i % 2

        @pl.when(i < 3)
        def _():
            ml(i + 1, 1 - s).start()

        ml(i, s).wait()
        back, dg, db = ln_back(gacc[pl.ds(r, 256), :], mid_v[s], sm_v[5:6, :])
        gm = g_v[pl.ds(r, 256), :].astype(F32) + back
        gacc[pl.ds(r, 256), :] = gm
        gb = gm.astype(BF16)
        g_v[pl.ds(r, 256), :] = gb
        sg_v[5:6, :] += dg
        sg_v[6:7, :] += db
        sg_v[4:5, :] += jnp.sum(gb.astype(F32), axis=0, keepdims=True)
        return c

    lax.fori_loop(0, 4, ln2, 0)
    for c in later + wpl:
        c.wait()
    for i in range(2):
        rows = slice(i * 512, (i + 1) * 512)
        st_v[0, i * 8:(i + 1) * 8] = dot(ot_v[rows, :], g_v[...]).astype(BF16).reshape(8, 64, D)
        w2_v[rows, :] = (dot(pre_v[6, rows, :], g_v[:, 0:512], 1, 1) + dot(pre_v[7, rows, :], g_v[:, 512:1024], 1, 1)).astype(BF16)

    def stp(j, k):
        return st_v.at[0, pl.ds(2 * chip(j) + k, 1)]

    def matep(j, c):
        sp.send(j, stp(j, 1 - core))
        return c

    def settlep(j, c):
        sp.settle(j, stp(j, core))
        return c

    lax.fori_loop(0, 8, matep, 0)
    s2.finish()
    s1.step(1)

    def stq(j, k):
        return st_v.at[:, 2 * chip(j) + k]

    def dqkv(g):
        c0, w = qcols[g]
        for j in range(3):
            for i in range(2):
                v = dot(w1_v[i * 512:(i + 1) * 512, :], qkvt_v[j, c0:c0 + w, :], 1, 1).astype(BF16)
                st_v[j, i * 8:(i + 1) * 8, :, c0:c0 + w] = v.reshape(8, 64, w)

        def send(j, c):
            sq[g].send(j, stq(j, 1 - core))
            return c

        lax.fori_loop(0, 8, send, 0)

    def settleq(g):
        def one(j, c):
            sq[g].settle(j, stq(j, core))
            return c

        lax.fori_loop(0, 8, one, 0)

    def begin_p():
        lax.fori_loop(0, 8, settlep, 0)
        sp.step(0)

    def free_a():
        s2.drain()
        pl.semaphore_signal(free.at[0], inc=1, device_id=here.partner(), device_id_type=MESH)
        for d in range(2):
            pl.semaphore_signal(free.at[1], inc=1, device_id=here.side(d), device_id_type=MESH)

    def first_q():
        for c in last:
            c.wait()
        pl.semaphore_wait(free.at[0], 1)
        dqkv(0)

    def begin_q():
        settleq(0)
        pl.semaphore_wait(free.at[1], 2)
        sq[0].step(0)

    def second_q():
        settleq(1)
        sq[1].step(0)

    events = {
        0: [begin_p],
        2: [lambda: s1.step(2), lambda: sp.step(1), free_a],
        6: [lambda: s1.step(3), lambda: sp.step(2)],
        7: [first_q],
        8: [begin_q, lambda: sp.step(3)],
        10: [s1.finish, lambda: sq[0].step(1)],
        11: [sp.finish, lambda: dqkv(1)],
        12: [second_q, lambda: sq[0].step(2)],
        14: [lambda: sq[1].step(1), lambda: sq[0].step(3)],
    }

    def hd(h, c):
        bwd_head(h, qkvt_v, ot_v, w2_v, lse_v)
        for n, fns in events.items():
            @pl.when(h == n)
            def _(fns=fns):
                for fn in fns:
                    fn()
        return c

    lax.fori_loop(0, 16, hd, 0)
    for c in wl:
        c.wait()

    def row(i):
        return pl.multiple_of((1 - i // 2) * yother + (i // 2) * ymine + (i % 2) * 256, 256)

    def xsend(i):
        at = pl.ds(pl.multiple_of(i * 256, 256), 256)
        return remote(w2_v.at[at, :], gxr_o.at[at, :], xsem.at[0, i], xsem.at[1, i], here.across())

    def xkeep(i):
        return pltpu.make_async_copy(mid_v.at[i], gx_o.at[pl.ds(i * 256, 256), :], xsem.at[2, i])

    def fin(i, c):
        r = row(i)
        up = None
        for j in range(3):
            for k in range(2):
                v = dot(qkvt_v[j, k * 512:(k + 1) * 512, pl.ds(r, 256)], pre_v[2 * j + k], 0, 1)
                up = v if up is None else up + v
        back, dg, db = ln_back(up, h_v[pl.ds(r, 256), :].astype(F32), sm_v[0:1, :])
        v = gacc[pl.ds(r, 256), :] + back
        sg_v[0:1, :] += dg
        sg_v[1:2, :] += db

        @pl.when(i < 2)
        def _():
            w2_v[pl.ds(pl.multiple_of((i % 2) * 256, 256), 256), :] = v.astype(BF16)
            xsend(i % 2).start()

        @pl.when(i >= 2)
        def _():
            mid_v[i % 2] = v
            xkeep(i % 2).start()

        return c

    lax.fori_loop(0, 2, fin, 0)
    dqkv(2)
    sq[1].step(2)
    ones = jnp.ones((16, T), BF16)
    for j, row in ((0, 2), (2, 3)):
        sg_v[row:row + 1, :] = dot(ones, qkvt_v[j], 1, 1)[0:1, :]
    settleq(2)
    sq[2].step(0)
    sq[0].finish()
    lax.fori_loop(2, 4, fin, 0)
    sg1 = remote(sg_v, sgm_v, ssem.at[0, 0], ssem.at[0, 1], here.partner())
    sg1.start()
    sq[2].step(1)
    sq[1].step(3)
    sg1.wait_recv()
    sg1.wait_send()
    sg_v[...] = sg_v[...] + sgm_v[...]
    b1g[...] = sg_v[8:16, 0:512]
    for j in range(8):
        t = chip(j)
        land_s[j, 0] = sg_v[0:8, pl.ds(pl.multiple_of(t * 128, 128), 128)]
        land_s[j, 1, 4:8, :] = jnp.zeros((4, 128), F32)
        fb = b1g[pl.ds(t, 1), :]
        for q in range(4):
            land_s[j, 1, q:q + 1, :] = fb[:, q * 128:(q + 1) * 128]
    ss_steps(ss, 0)
    ss_steps(ss, 1)
    sq[2].step(2)
    ss_steps(ss, 2)
    sq[1].finish()
    ss_steps(ss, 3)
    sq[2].step(3)
    for d in range(2):
        ss_ring(ss, d, 3).wait_recv()
    fold(land_s.at[7], rb_s.at[0, 3], rb_s.at[1, 3])
    sg2 = remote(land_s.at[7], sgy_v, ssem.at[1, 0], ssem.at[1, 1], here.across())
    sg2.start()
    sq[2].finish()
    sg2.wait_recv()
    sg2.wait_send()
    fold(land_s.at[7], sgy_v)
    skeep = pltpu.make_async_copy(land_s.at[7], sg_o, ssem.at[2, 0])
    skeep.start()
    for s in range(4):
        for d in range(2):
            ss_ring(ss, d, s).wait_send()
    skeep.wait()
    for i in range(2):
        xsend(i).wait()
        xkeep(i).wait()
    osend.wait()
    for s in (s1, sp, *sq):
        s.drain()
    for s in (s2, s1, sp, *sq):
        s.arrive()


def ss_ring(ss, d, s):
    if s == 0:
        src, dst = ss.land.at[0, d], ss.rb.at[d, 0, d]
    else:
        src, dst = ss.land.at[2 * s - 1 + d], ss.rb.at[d, s]
    return remote(src, dst, ss.rsem.at[0, d, s], ss.rsem.at[1, d, s], ss.pl.side(d))


def ss_steps(ss, s):
    for d in range(2):
        if s:
            ss_ring(ss, d, s - 1).wait_recv()
            j = 2 * s - 1 + d
            if s == 1:
                ss.land[j, d] = ss.land[j, d] + ss.rb[d, 0, d]
            else:
                fold(ss.land.at[j], ss.rb.at[d, s - 1])
        ss_ring(ss, d, s).start()


def bwd_call(size):
    dma = pltpu.SemaphoreType.DMA
    block = S((4, 64, D), BF16)
    return pl.pallas_call(
        functools.partial(bwd_body, size),
        name="backward",
        in_specs=[pl.BlockSpec(memory_space=pltpu.SMEM)] + [ANY] * 17,
        out_specs=[ANY] * 12,
        out_shape=[S((T // 2, D), BF16), S((T // 2, D), F32), S((T // 2, D), BF16), block, block, block, block,
                   S((1, 64, D), BF16), S((1, 64, D), BF16), S((3, 64, D), BF16), S((3, 64, D), BF16), S((2, 8, 128), F32)],
        scratch_shapes=[V((T, D), BF16), V((T, D), BF16), V((T, D), F32), V((T, 1024), BF16), V((NTILE, T, 512), BF16), V((D, 1024), BF16), V((1024, D), BF16),
                        V((8, 512), F32), V((2, 256, D), F32), V((3, D, T), BF16), V((D, T), BF16), V((16, T), F32), V((16, D), F32), V((16, D), F32),
                        V((16, D), F32), V((2, 8, 128), F32),
                        V((3, 16, 64, D), BF16), V((8, 4, 64, D), BF16), V((8, 4, 64, D), BF16), V((8, 1, 64, D), BF16), V((8, 2, 8, 128), F32),
                        V((2, 4, 4, 64, D), BF16), V((2, 4, 4, 64, D), BF16), V((2, 4, 1, 64, D), BF16), V((2, 4, 2, 8, 128), F32),
                        dma((9,)), dma((2, 4)), dma((8,)), dma((2,)), dma((3, 2)), dma((8, 2, 8)), dma((9, 2, 2, 4)), dma((8, 3)), dma((3, 2)), dma((1, 2)),
                        pltpu.SemaphoreType.REGULAR((2,))],
        compiler_params=pltpu.CompilerParams(vmem_limit_bytes=67043328, collective_id=1, has_side_effects=True),
    )


def fast_body(clips, cotangent, valid, *shards):
    size = lax.axis_size("fsdp")
    me = lax.axis_index("fsdp")
    mine = lax.axis_index("seq")
    (g1, b1, wq, wk, wv, bq, bv, wp, bp, g2, b2, w1, fb1, w2, fb2) = shards
    n, m = g1.shape[0], fb1.shape[0]
    vecs = jnp.stack([g1, b1, bq, bv, bp, g2, b2, fb2])
    sml = lax.dynamic_update_slice(jnp.zeros((8, D), vecs.dtype), vecs, (0, me * n))
    fsm = lax.dynamic_update_slice(jnp.zeros((FF,), vecs.dtype), fb1, (me * m,)).reshape(-1, D)
    sml = jnp.concatenate([sml, fsm, jnp.zeros((8 - FF // D, D), vecs.dtype)])
    out, cot_in, x, sm, wqkv, wp_all, w1_all, w2_all, *saved = fwd_call(size, T, D, FF)(clips, cotangent, sml, wq, wk, wv, wp, w1, w2)
    out_in, gx, gx_in, dw2, dw2y, dw1, dw1y, dwp, dwpy, dq, dqy, sg = bwd_call(size)(
        valid, cotangent, cot_in, out, x, sm, wqkv, wp_all, w1_all, w2_all, *saved)

    def both(a, b):
        return a.astype(F32) + b.astype(F32)

    def halves(own, other):
        return jnp.where(mine == 0, jnp.stack([own, other]), jnp.stack([other, own]))

    dw2 = both(dw2, dw2y).reshape(-1, D)
    dw1 = both(dw1, dw1y).transpose(1, 0, 2).reshape(n, -1)
    dq = both(dq, dqy)
    dwp = both(dwp, dwpy)[0]
    own = lax.dynamic_slice(sg[0], (0, me % 2 * n), (8, n))
    dfb1 = lax.dynamic_slice(sg[1, 0:4].reshape(-1), (me % 2 * m,), (m,))
    out = halves(lax.dynamic_slice(out, (mine * (T // 2), 0), (T // 2, D)), out_in)
    gx = halves(gx, gx_in.astype(F32))
    return (out, gx, own[0], own[1], dq[0], dq[1], dq[2], own[2], own[3], dwp, own[4], own[5], own[6], dw1, dfb1, dw2, own[7])


def solution(mesh):
    in_specs = (
        P("fsdp", "seq", None),
        P("fsdp", "seq", None),
        P("fsdp"),
        P("fsdp"),
        P("fsdp"),
        P("fsdp", None),
        P("fsdp", None),
        P("fsdp", None),
        P("fsdp"),
        P("fsdp"),
        P("fsdp", None),
        P("fsdp"),
        P("fsdp"),
        P("fsdp"),
        P("fsdp", None),
        P("fsdp"),
        P("fsdp", None),
        P("fsdp"),
    )
    out_specs = (
        P("fsdp", "seq", None),
        P("fsdp", "seq", None),
        P("fsdp"),
        P("fsdp"),
        P("fsdp", None),
        P("fsdp", None),
        P("fsdp", None),
        P("fsdp"),
        P("fsdp"),
        P("fsdp", None),
        P("fsdp"),
        P("fsdp"),
        P("fsdp"),
        P("fsdp", None),
        P("fsdp"),
        P("fsdp", None),
        P("fsdp"),
    )
    quick = mesh.shape["seq"] == 2 and mesh.shape["fsdp"] == 16
    return jax.shard_map(fast_body if quick else body, mesh=mesh, in_specs=in_specs, out_specs=out_specs, check_vma=False)
```

profile of v0, /device:TPU:0, one launch (start us, length us, event | category | flops | bytes accessed | tf_op | source)
XLA Modules:
  0.0 353.7 jit_solution(15625689310081668234)
XLA Ops:
  0.7 0.8 stack.66
  1.5 0.2 dynamic_update_slice.6
  1.6 0.9 dynamic_update_slice.7
  2.5 0.1 pad.10.clone
  2.6 0.7 maximum_maximum_fusion.sml
  3.3 149.8 %forward.1 = (bf16[1024,1024]{1,0:T(8,128)(2,1)}, bf16[512,1024]{1,0:T(8,128)(2,1)}, bf16[1024,1024]{1,0:T(8,128)(2,1)}, f32[16,1024]{1,0:T(8,128)}, bf16[3,1024...) custom-call(bf16[2,512,1024]{2,1,0:T(8,128)(2,1)} %clips.1, ...), custom_call_target="tpu_custom_call" | custom-call | tf_op jit(solution)/shard_map/forward/pallas_call | solution.py:1397
  153.1 185.2 %backward.1 = (bf16[512,1024]{1,0:T(8,128)(2,1)}, f32[512,1024]{1,0:T(8,128)}, bf16[512,1024]{1,0:T(8,128)(2,1)}, bf16[4,64,1024]{2,1,0:T(8,128)(2,1)}, bf16[4,6...) custom-call(s32[2]{0:T(128)} %valid.1, ...), custom_call_target="tpu_custom_call" | custom-call | tf_op jit(solution)/shard_map/backward/pallas_call | solution.py:1398
  338.3 2.4 convert_add_fusion
  340.8 0.0 copy-done.3
  340.8 0.2 add_bitcast_fusion
  341.0 1.1 copy.36
  342.1 0.1 convert_add_fusion.1
  342.2 0.0 copy-done.6
  342.2 0.0 copy-done.7
  342.2 1.0 slice_bitcast_fusion
  343.2 0.4 copy-done.1
  343.6 0.2 bitcast_convert_fusion
  343.9 5.1 %maximum_select_fusion = f32[2,512,1024]{2,1,0:T(8,128)} fusion(f32[1,512,1024]{2,1,0:T(8,128)S(1)} %bitcast_convert_fusion, f32[1,512,1024]{2,1,0:T(8,128)} %bitcast.46, pred[]{:T(512)S(6)} %eq.7), kind=kLoop, calls=%fused_computation | loop fusion | flops 3145728 | bytes 8388609 | tf_op jit(solution)/shard_map/jit(_where)/select_n | solution.py:1405
  349.0 1.4 dynamic-slice_bitcast_fusion
  350.4 0.2 copy-done
  350.5 1.6 maximum_select_fusion.1
  352.2 0.1 constant_dynamic-slice_fusion
  352.3 0.5 slice_bitcast_fusion.4
  352.8 0.6 dynamic_slice.11
  (19 shorter events, 0.1 us)
Async XLA Ops:
  338.3 2.5 copy-start.2
  338.3 2.5 copy-start.3
  340.8 1.3 copy-start.4
  340.8 1.3 copy-start.5
  341.0 1.2 copy-start.6
  341.0 1.2 copy-start.7
  342.1 1.6 copy-start.1
  349.0 1.5 copy-start
  350.5 1.6 copy-start.8
where the time goes:
time: 358 us; the launch traced here: 354 us
  Pallas kernels  335 us (94%)
  other arithmetic  11.4 us (3%)
  local copies, waits for them, and re-layouts  6.26 us (2%)
    pallas_call x1, Pallas kernels, fast_body(): bwd_call(size)  185 us
    pallas_call x1, Pallas kernels, fast_body(): fwd_call(size, T, D, FF)(clips, cotangent, sml, wq, wk, wv, wp, w1, w2)  150 us

commit v1 on v0

--- a/solution.py
+++ b/solution.py
@@ -802,21 +802,31 @@
         at = pl.ds(pl.multiple_of(t * tile, tile), tile)
         return pltpu.make_async_copy(w2_v.at[at, :], w2_o.at[at, :], tsem.at[2, j])
 
-    for j, off in enumerate(order):
-        t = here.chip(off)
+    def turn(j):
+        odd = j % 2
+        return here.chip((1 - odd) * (j // 2) - odd * ((j + 1) // 2))
+
+    def mlp_tile(j, c):
+        t = turn(j)
         slot = j % 2
-        if j % 2 == 1:
-            g2.step_over(j // 2)
-            if j // 2 < g2.last:
-                g2.step(j // 2 + 1)
-            g2.step_mate(j // 2)
+        for k in range(g2.last + 1):
+            @pl.when(j == 2 * k + 1)
+            def _(k=k):
+                g2.step_over(k)
+                if k < g2.last:
+                    g2.step(k + 1)
+                g2.step_mate(k)
+
         wcp(j, t).start()
-        if j >= 2:
+
+        @pl.when(j >= 2)
+        def _():
             for k in range(2):
-                tcp(k, slot, here.chip(order[j - 2])).wait()
+                tcp(k, slot, turn(j - 2)).wait()
+
         col = pl.multiple_of(t * tile, tile)
 
-        def mlp(i, c, t=t, slot=slot, col=col):
+        def mlp(i, c):
             r = pl.multiple_of(i * 512, 512)
             u = dot(n2[pl.ds(r, 512), :], w1_v[:, pl.ds(col, tile)]) + b1_v[pl.ds(t, 1), :]
             cdf = 0.5 + 0.5 * lax.erf(u * root_half)
@@ -829,6 +839,9 @@
         lax.fori_loop(0, T // 512, mlp, 0)
         for k in range(2):
             tcp(k, slot, t).start()
+        return c
+
+    lax.fori_loop(0, len(order), mlp_tile, 0)
     for j in range(len(order) - 2, len(order)):
         for k in range(2):
             tcp(k, j % 2, here.chip(order[j])).wait()
@@ -1184,10 +1197,14 @@
 
     def dqkv(g):
         c0, w = qcols[g]
-        for j in range(3):
-            for i in range(2):
-                v = dot(w1_v[i * 512:(i + 1) * 512, :], qkvt_v[j, c0:c0 + w, :], 1, 1).astype(BF16)
-                st_v[j, i * 8:(i + 1) * 8, :, c0:c0 + w] = v.reshape(8, 64, w)
+
+        def product(k, c):
+            j, i = k // 2, k % 2
+            v = dot(w1_v[pl.ds(pl.multiple_of(i * 512, 512), 512), :], qkvt_v[j, c0:c0 + w, :], 1, 1).astype(BF16)
+            st_v[j, pl.ds(i * 8, 8), :, c0:c0 + w] = v.reshape(8, 64, w)
+            return c
+
+        lax.fori_loop(0, 6, product, 0)
 
         def send(j, c):
             sq[g].send(j, stq(j, 1 - core))
@@ -1402,7 +1419,7 @@
         return a.astype(F32) + b.astype(F32)
 
     def halves(own, other):
-        return jnp.where(mine == 0, jnp.stack([own, other]), jnp.stack([other, own]))
+        return jnp.where(lax.broadcasted_iota(jnp.int32, (2, 1, 1), 0) == mine, own[None], other[None])
 
     dw2 = both(dw2, dw2y).reshape(-1, D)
     dw1 = both(dw1, dw1y).transpose(1, 0, 2).reshape(n, -1)

time: 358 us -> 343 us (0.958)
  Pallas kernels: 335 us -> 325 us
    pallas_call x1, Pallas kernels: 185 us -> 175 us  [fast_body(): bwd_call(size)]
where the time goes in v1:
time: 343 us; the launch traced here: 342 us
  Pallas kernels  325 us (95%)
  other arithmetic  10.5 us (3%)
  local copies, waits for them, and re-layouts  6.26 us (2%)
    pallas_call x1, Pallas kernels, fast_body(): bwd_call(size)  175 us
    pallas_call x1, Pallas kernels, fast_body(): fwd_call(size, T, D, FF)(clips, cotangent, sml, wq, wk, wv, wp, w1, w2)  150 us

profile of v1, /device:TPU:0, one launch (start us, length us, event | category | flops | bytes accessed | tf_op | source)
XLA Modules:
  0.0 342.2 jit_solution(4867352097324845430)
XLA Ops:
  0.7 0.8 stack.35
  1.5 0.2 dynamic_update_slice.6
  1.6 0.9 dynamic_update_slice.7
  2.5 0.1 pad.2.clone
  2.6 0.7 maximum_maximum_fusion.sml
  3.3 150.0 %forward.1 = (bf16[1024,1024]{1,0:T(8,128)(2,1)}, bf16[512,1024]{1,0:T(8,128)(2,1)}, bf16[1024,1024]{1,0:T(8,128)(2,1)}, f32[16,1024]{1,0:T(8,128)}, bf16[3,1024...) custom-call(bf16[2,512,1024]{2,1,0:T(8,128)(2,1)} %clips.1, ...), custom_call_target="tpu_custom_call" | custom-call | tf_op jit(solution)/shard_map/forward/pallas_call | solution.py:1414
  153.3 174.6 %backward.1 = (bf16[512,1024]{1,0:T(8,128)(2,1)}, f32[512,1024]{1,0:T(8,128)}, bf16[512,1024]{1,0:T(8,128)(2,1)}, bf16[4,64,1024]{2,1,0:T(8,128)(2,1)}, bf16[4,6...) custom-call(s32[2]{0:T(128)} %valid.1, ...), custom_call_target="tpu_custom_call" | custom-call | tf_op jit(solution)/shard_map/backward/pallas_call | solution.py:1415
  328.0 2.4 convert_add_fusion
  330.4 0.0 copy-done.3
  330.4 0.2 add_bitcast_fusion
  330.6 1.1 copy.36
  331.7 0.1 convert_add_fusion.1
  331.8 0.0 copy-done.6
  331.8 0.0 copy-done.7
  331.8 1.0 slice_bitcast_fusion
  332.8 0.4 copy-done.1
  333.3 0.2 convert_element_type.27
  333.5 4.3 %broadcast_select_fusion = f32[2,512,1024]{2,1,0:T(8,128)} fusion(f32[512,1024]{1,0:T(8,128)S(1)} %convert_element_type.27, f32[512,1024]{1,0:T(8,128)} %get-tuple-element.62, pred[2]{0:T(512)(128)(4,1)S(1)} %iota_compare_fusion), kind=kLoop, calls=%fused_computation | loop fusion | flops 1048576 | bytes 8388610 | tf_op jit(solution)/shard_map/jit(_where)/select_n | solution.py:1422
  337.8 1.4 constant_dynamic-slice_fusion.1
  339.2 0.2 copy-done
  339.4 1.6 broadcast_select_fusion.1
  341.0 0.1 constant_dynamic-slice_fusion
  341.0 0.5 slice_bitcast_fusion.4
  341.6 0.6 dynamic_slice.11
  (20 shorter events, 0.1 us)
Async XLA Ops:
  327.9 2.5 copy-start.2
  328.0 2.5 copy-start.3
  330.4 1.3 copy-start.4
  330.4 1.3 copy-start.5
  330.6 1.2 copy-start.6
  330.6 1.2 copy-start.7
  331.7 1.6 copy-start.1
  337.8 1.5 copy-start
  339.4 1.6 copy-start.8
